TPU v7x, 32 devices: a whole 2x2x4 slice. The times are simulated.
32 devices in a mesh: old: 8 (over z, core), new: 4 (over y, x).
Axes of the slice: x: 2, y: 2, z: 4, core: 2. Of those that a mesh axis runs over, the one named last changes fastest.
Arguments:
- centroids_old: bfloat16 [65536, 768], P(('old', 'new')), may hold values from -6 to 6
- centroids_new: bfloat16 [16384, 768], P(('old', 'new')), may hold values from -6 to 6
- mass_old: float32 [65536], P(('old', 'new')), may hold values from 0.5 to 18
- mass_new: float32 [16384], P(('old', 'new')), may hold values from 0.5 to 18
- pairs: int32 [256, 8], P(('old', 'new')), may hold values from 0 to 63, as said below
Outputs:
- log_old: float32 [65536], P(('old', 'new'))
- log_new: float32 [16384], P(('old', 'new'))
Inputs may be any that keep to these rules, and one draw needn't show every extreme that they name: `pairs`: each row names 8 different new blocks, all held by devices with the same index along old as the device that holds that old block. The rows held by one device name, of the blocks of each such device, exactly 2 different blocks. Every new block is named by some row.
All inputs are finite; a program needn't handle non-finite values.
Results may differ from a plain program's by a relative error of at most 0.0003.
Values may be sent and summed in bfloat16 or wider, within the bound.
A program may use at most 128 MiB of HBM per device.

v0:
```python
import functools
import math

import jax
import jax.numpy as jnp
from jax import lax
from jax.experimental import pallas as pl
from jax.experimental.pallas import tpu as pltpu
from jax.sharding import PartitionSpec as P

D = 768
CENTROID_BLOCK = 256
PARTNER_BLOCKS = 8
ITERS = 3


ENTROPY_SCALE = 0.025


def row_norm_values(blocks):
    return jnp.sqrt(jnp.sum(jnp.square(blocks.astype(jnp.float32)), axis=-1) + 1e-06)


def general_body(centroids_old, centroids_new, mass_old, mass_new, pairs):
    owners = lax.axis_size("new")
    my_old = lax.axis_index("old")
    old_count = centroids_old.shape[0] // CENTROID_BLOCK
    new_count = centroids_new.shape[0] // CENTROID_BLOCK
    devices_all = lax.axis_size("old") * owners
    totals = lax.psum((jnp.sum(mass_old), jnp.sum(mass_new)), ("old", "new"))
    rel_old = (mass_old * (mass_old.shape[0] * devices_all / totals[0])).reshape(
        old_count, CENTROID_BLOCK
    )
    rel_new = (mass_new * (mass_new.shape[0] * devices_all / totals[1])).reshape(
        new_count, CENTROID_BLOCK
    )
    old_blocks = centroids_old.reshape(old_count, CENTROID_BLOCK, D)
    previous_norm = row_norm_values(old_blocks)
    local_ids = pairs - my_old * (owners * new_count)
    everyone = lax.all_gather(centroids_new, "new", axis=0, tiled=True).reshape(
        owners * new_count, CENTROID_BLOCK, D
    )
    norm_all = row_norm_values(everyone)
    chosen = everyone[local_ids]
    selected_norm = norm_all[local_ids]
    columns = owners * new_count
    inner_products = jnp.einsum(
        "rbd,rkcd->rkbc", old_blocks, chosen, preferred_element_type=jnp.float32
    )
    kernel = jnp.exp(
        inner_products
        / (previous_norm[:, None, :, None] * selected_norm[:, :, None, :])
        / ENTROPY_SCALE
    ) * (1.0 / (PARTNER_BLOCKS * CENTROID_BLOCK))
    selector = (local_ids.reshape(-1)[:, None] == jnp.arange(columns)[None, :]).astype(jnp.float32)
    scales = jnp.ones((new_count, CENTROID_BLOCK), jnp.float32)
    left_scale = jnp.ones((old_count, CENTROID_BLOCK), jnp.float32)
    for sweep_index in range(ITERS):
        if sweep_index == 0:
            picked = jnp.ones((old_count, PARTNER_BLOCKS, CENTROID_BLOCK), jnp.float32)
        else:
            fetched = lax.all_gather(scales, "new", axis=0, tiled=True)
            picked = fetched[local_ids]
        row_sum = jnp.einsum("ikbc,ikc->ib", kernel, picked, precision=lax.Precision.HIGHEST)
        left_scale = rel_old / row_sum
        col_terms = jnp.einsum("ikbc,ib->ikc", kernel, left_scale, precision=lax.Precision.HIGHEST)
        gathered_terms = jnp.dot(
            selector.T,
            col_terms.reshape(-1, CENTROID_BLOCK),
            precision=lax.Precision.HIGHEST,
            preferred_element_type=jnp.float32,
        )
        column = lax.psum_scatter(gathered_terms, "new", scatter_dimension=0, tiled=True)
        scales = rel_new / column
    return (jnp.log(left_scale).reshape(-1), jnp.log(scales).reshape(-1))


MESH = pl.DeviceIdType.MESH
LANES = 128
SUBLANES = 8
TILE = 256
STAGE_TILE = 512
UNROLL = 4


def eye_mask():
    shape = (LANES, LANES)
    return lax.broadcasted_iota(jnp.int32, shape, 0) == lax.broadcasted_iota(jnp.int32, shape, 1)


def to_row(column, eye):
    wide = jnp.broadcast_to(column, (LANES, LANES))
    return jnp.sum(jnp.where(eye, wide, 0.0), axis=0, keepdims=True)


def to_column(row, eye):
    wide = jnp.broadcast_to(row, (LANES, LANES))
    return jnp.sum(jnp.where(eye, wide, 0.0), axis=1, keepdims=True)


def dense_kernel(
    olds,
    devices_all,
    old_hbm,
    new_hbm,
    mass_old_ref,
    mass_new_ref,
    left_ref,
    scales_ref,
    a_ref,
    b_ref,
    k_ref,
    inv_old,
    mass_wide,
    row_acc,
    u_ref,
    col_acc,
    v_ref,
    rel_new,
    meta,
    meta_in,
    sums,
    sums_in,
    cols,
    cols_in,
    load_sem,
    gather_send,
    gather_recv,
    meta_send,
    meta_recv,
    sums_send,
    sums_recv,
    cols_send,
    cols_recv,
):
    me = lax.axis_index("new")
    my_old = lax.axis_index("old")
    flip_x = 1 - 2 * lax.rem(me, 2)
    flip_y = 2 - 4 * lax.div(me, 2)
    peers = (None, me + flip_x, me + flip_y, me + flip_x + flip_y)
    old_steps = olds.bit_length() - 1
    old_peers = [
        my_old + (1 << k) - (2 << k) * lax.rem(lax.div(my_old, 1 << k), 2) for k in range(old_steps)
    ]

    n_old = a_ref.shape[0]
    half = b_ref.shape[2]
    depth = a_ref.shape[1]
    r = mass_new_ref.shape[0]
    tiles = n_old // TILE
    per_tile = TILE // LANES
    per_half = half // LANES
    scale = float(PARTNER_BLOCKS * CENTROID_BLOCK)
    eye = eye_mask()

    load_a = pltpu.make_async_copy(old_hbm, a_ref, load_sem.at[0])
    load_b = [
        pltpu.make_async_copy(new_hbm.at[h], b_ref.at[0, h], load_sem.at[1 + h]) for h in range(2)
    ]
    load_a.start()
    for copy in load_b:
        copy.start()

    meta[...] = jnp.zeros_like(meta)
    meta[0:r, :] = mass_new_ref[...]
    meta[r : r + 1, :] = jnp.sum(mass_old_ref[...], axis=0, keepdims=True)

    barrier = pltpu.get_barrier_semaphore()
    for p in range(1, 4):
        pl.semaphore_signal(barrier, inc=1, device_id={"new": peers[p]}, device_id_type=MESH)
    for peer in old_peers:
        pl.semaphore_signal(barrier, inc=1, device_id={"old": peer}, device_id_type=MESH)
    pl.semaphore_wait(barrier, 3 + len(old_peers))

    meta_copies = [
        pltpu.make_async_remote_copy(
            src_ref=meta,
            dst_ref=meta_in.at[p - 1],
            send_sem=meta_send.at[p - 1],
            recv_sem=meta_recv.at[p - 1],
            device_id={"new": peers[p]},
            device_id_type=MESH,
        )
        for p in range(1, 4)
    ]
    for copy in meta_copies:
        copy.start()

    def send(index, src, slot, h, p, part=None):
        return pltpu.make_async_remote_copy(
            src_ref=src,
            dst_ref=b_ref.at[slot, h] if part is None else b_ref.at[slot, h, part],
            send_sem=gather_send.at[index],
            recv_sem=gather_recv.at[index],
            device_id={"new": peers[p]},
            device_id_type=MESH,
        )

    moves = [
        send(0, new_hbm.at[1], 1, 1, 1),
        send(1, new_hbm.at[0], 1, 0, 1),
        send(2, new_hbm.at[0], 2, 0, 2),
        send(3, new_hbm.at[1], 2, 1, 2),
    ]
    quarters = [pl.ds(q * (half // 2), half // 2) for q in range(2)]
    relay_x = [send(4 + q, b_ref.at[2, 0, quarters[q]], 3, 0, 1, quarters[q]) for q in range(2)]
    relay_y = [send(6 + q, b_ref.at[1, 1, quarters[q]], 3, 1, 2, quarters[q]) for q in range(2)]
    for index in (0, 2, 1, 3):
        moves[index].start()

    load_a.wait()

    @pl.loop(0, tiles)
    def _(t):
        rows = pl.ds(pl.multiple_of(t * TILE, TILE), TILE)
        a = a_ref[rows, :].astype(jnp.float32)
        total = jnp.sum(a * a, axis=1, keepdims=True)
        inv_old[rows, :] = jnp.broadcast_to(1.0 / jnp.sqrt(total + 1e-06), (TILE, LANES))
        for i in range(per_tile):
            part = pl.ds(pl.multiple_of(t * TILE + i * LANES, LANES), LANES)
            column = to_column(mass_old_ref[pl.ds(t * per_tile + i, 1), :], eye)
            mass_wide[part, :] = jnp.broadcast_to(column * scale, (LANES, LANES))

    def stage(chunks, first, start=0, width=None):
        width = half if width is None else width
        factors = []
        for slot, h in chunks:
            b = b_ref[slot, h, start : start + width].astype(jnp.float32)
            total = jnp.sum(b * b, axis=1, keepdims=True)
            inverse = (math.log2(math.e) / ENTROPY_SCALE) / jnp.sqrt(total + 1e-06)
            factors.append(
                [to_row(inverse[j : j + LANES], eye) for j in range(0, width, LANES)]
            )

        @pl.loop(0, n_old // STAGE_TILE)
        def _(t):
            rows = pl.ds(pl.multiple_of(t * STAGE_TILE, STAGE_TILE), STAGE_TILE)
            a = a_ref[rows, :]
            inv = inv_old[rows, :]
            acc = jnp.zeros((STAGE_TILE, LANES), jnp.float32) if first else row_acc[rows, :]
            for some in [chunks] if width < half else [(chunk,) for chunk in chunks]:
                blocks = [b_ref[slot, h, start : start + width] for slot, h in some]
                products = lax.dot_general(
                    a,
                    jnp.concatenate(blocks, axis=0) if len(blocks) > 1 else blocks[0],
                    (((1,), (1,)), ((), ())),
                    preferred_element_type=jnp.float32,
                )
                for i, (slot, h) in enumerate(some):
                    factor = factors[chunks.index((slot, h))]
                    for j in range(0, width, LANES):
                        part = products[:, i * width + j : i * width + j + LANES]
                        k = jnp.exp2(part * inv * factor[j // LANES])
                        k_ref[2 * slot + h, rows, start + j : start + j + LANES] = k
                        acc = acc + k
            row_acc[rows, :] = acc

    for copy in load_b:
        copy.wait()
    for copy in meta_copies:
        copy.wait()
    old_sum = meta[r : r + 1, :]
    new_sum = jnp.sum(meta[0:r, :], axis=0, keepdims=True)
    for p in range(1, 4):
        old_sum = old_sum + meta_in[p - 1, r : r + 1, :]
        new_sum = new_sum + jnp.sum(meta_in[p - 1, 0:r, :], axis=0, keepdims=True)
    sums[0] = jnp.zeros((SUBLANES, LANES), jnp.float32)
    sums[0, 0:1, :] = old_sum
    sums[0, 1:2, :] = new_sum
    sums_copies = [
        pltpu.make_async_remote_copy(
            src_ref=sums.at[k],
            dst_ref=sums_in.at[k],
            send_sem=sums_send.at[k],
            recv_sem=sums_recv.at[k],
            device_id={"old": peer},
            device_id_type=MESH,
        )
        for k, peer in enumerate(old_peers)
    ]

    def advance(k):
        sums_copies[k].wait()
        sums[k + 1] = sums[k] + sums_in[k]
        if k + 1 < old_steps:
            sums_copies[k + 1].start()

    sums_copies[0].start()
    stage(((0, 0), (0, 1)), True)
    moves[0].wait_recv()
    for copy in relay_y:
        copy.start()
    moves[2].wait_recv()
    for copy in relay_x:
        copy.start()
    advance(0)
    stage(((1, 1), (2, 0)), False)
    advance(1)
    moves[1].wait_recv()
    moves[3].wait_recv()
    stage(((1, 0), (2, 1)), False)
    rel_new[0] = meta[0:r, :] * scale
    for p in range(1, 4):
        rel_new[p] = meta_in[p - 1, 0:r, :] * scale
    for piece in range(2):
        relay_x[piece].wait_recv()
        relay_y[piece].wait_recv()
        stage(((3, 0), (3, 1)), False, piece * (half // 2), half // 2)
    for move in moves + relay_x + relay_y:
        move.wait_send()

    my_x, my_y = lax.rem(me, 2), lax.div(me, 2)

    def slot_of(owner):
        x = 1 - my_x if owner % 2 else my_x
        y = 1 - my_y if owner // 2 else my_y
        return x + 2 * y

    def col_sums(slot):
        @pl.loop(0, tiles // UNROLL, init_carry=[jnp.zeros((SUBLANES, LANES), jnp.float32)] * r)
        def sums_of(t, carry):
            for b in range(UNROLL):
                start = (t * UNROLL + b) * TILE
                rows = pl.ds(pl.multiple_of(start, TILE), TILE)
                u = u_ref[rows, :]
                new = []
                for g in range(r):
                    c, j = 2 * slot + g // per_half, g % per_half
                    part = k_ref[c, rows, j * LANES : (j + 1) * LANES] * u
                    part = part.reshape(TILE // SUBLANES, SUBLANES, LANES)
                    new.append(carry[g] + jnp.sum(part, axis=0))
                carry = new
            return carry

        for g in range(r):
            col_acc[g] = sums_of[g]
        return jnp.sum(col_acc[...], axis=1)

    def add_rows(slot, owner, first):
        @pl.loop(0, tiles // UNROLL)
        def _(t):
            for b in range(UNROLL):
                start = (t * UNROLL + b) * TILE
                rows = pl.ds(pl.multiple_of(start, TILE), TILE)
                acc = jnp.zeros((TILE, LANES), jnp.float32) if first else row_acc[rows, :]
                for g in range(r):
                    c, j = 2 * slot + g // per_half, g % per_half
                    weights = v_ref[owner, g : g + 1, :]
                    acc = acc + k_ref[c, rows, j * LANES : (j + 1) * LANES] * weights
                row_acc[rows, :] = acc

    def exchange(sweep, index, p, src):
        return pltpu.make_async_remote_copy(
            src_ref=cols.at[sweep, src],
            dst_ref=cols_in.at[sweep, p - 1, index],
            send_sem=cols_send.at[sweep, p - 1, index],
            recv_sem=cols_recv.at[sweep, p - 1, index],
            device_id={"new": peers[p]},
            device_id_type=MESH,
        )

    for sweep in range(ITERS):
        last = sweep == ITERS - 1

        @pl.loop(0, n_old // STAGE_TILE)
        def _(t):
            rows = pl.ds(pl.multiple_of(t * STAGE_TILE, STAGE_TILE), STAGE_TILE)
            row_sum = jnp.sum(row_acc[rows, :], axis=1, keepdims=True)
            u_ref[rows, :] = mass_wide[rows, :] / jnp.broadcast_to(row_sum, (STAGE_TILE, LANES))

        if last:
            copies = []
            for p in (3, 2, 1):
                cols[sweep, p] = col_sums(p)
                copies.append(exchange(sweep, 0, p, p))
                copies[-1].start()
            total = col_sums(0)
            for k in range(2, old_steps):
                advance(k)
            totals = jnp.sum(sums[old_steps], axis=1, keepdims=True)
            alpha = n_old * devices_all / totals[0:1, :]
            beta = r * LANES * devices_all / totals[1:2, :]
            ratio = alpha / beta
            left_factor, scales_factor = alpha, 1.0 / ratio
            for _ in range(ITERS - 1):
                left_factor, scales_factor = left_factor * ratio, scales_factor / ratio
            for i in range(n_old // LANES):
                left_ref[i : i + 1, :] = (
                    to_row(u_ref[i * LANES : (i + 1) * LANES, :], eye) * left_factor
                )
            for copy in copies:
                copy.wait()
            for p in range(1, 4):
                total = total + cols_in[sweep, p - 1, 0]
            scales_ref[...] = rel_new[0] / total * scales_factor
        else:
            copies = []
            for owner in range(4):
                cols[sweep, owner] = col_sums(slot_of(owner))
                copies.append([exchange(sweep, owner, p, owner) for p in (3, 2, 1)])
                for copy in copies[-1]:
                    copy.start()
            for owner in range(4):
                for copy in copies[owner]:
                    copy.wait()
                slot = slot_of(owner)
                total = cols[sweep, owner]
                for p in range(1, 4):
                    total = total + cols_in[sweep, p - 1, owner]
                v_ref[owner] = rel_new[slot] / total
                add_rows(slot, owner, owner == 0)


def log_kernel(left_ref, scales_ref, log_old_ref, log_new_ref):
    log_old_ref[...] = jnp.log(left_ref[...])
    log_new_ref[...] = jnp.log(scales_ref[...])


def dense_body(mesh, centroids_old, centroids_new, mass_old, mass_new):
    owners = mesh.shape["new"]
    olds = mesh.shape["old"]
    n_old, depth = centroids_old.shape
    n_new = centroids_new.shape[0]
    half = n_new // 2
    r = n_new // LANES
    old_steps = olds.bit_length() - 1
    f32 = jnp.float32
    meta_rows = -(-(r + 1) // SUBLANES) * SUBLANES
    left, scales = pl.pallas_call(
        functools.partial(dense_kernel, olds, olds * owners),
        out_shape=(
            jax.ShapeDtypeStruct((n_old // LANES, LANES), f32),
            jax.ShapeDtypeStruct((r, LANES), f32),
        ),
        in_specs=[
            pl.BlockSpec(memory_space=pl.ANY),
            pl.BlockSpec(memory_space=pl.ANY),
            pl.BlockSpec(memory_space=pltpu.VMEM),
            pl.BlockSpec(memory_space=pltpu.VMEM),
        ],
        out_specs=(
            pl.BlockSpec(memory_space=pltpu.VMEM),
            pl.BlockSpec(memory_space=pltpu.VMEM),
        ),
        scratch_shapes=[
            pltpu.VMEM((n_old, depth), jnp.bfloat16),
            pltpu.VMEM((owners, 2, half, depth), jnp.bfloat16),
            pltpu.VMEM((2 * owners, n_old, half), f32),
            pltpu.VMEM((n_old, LANES), f32),
            pltpu.VMEM((n_old, LANES), f32),
            pltpu.VMEM((n_old, LANES), f32),
            pltpu.VMEM((n_old, LANES), f32),
            pltpu.VMEM((r, SUBLANES, LANES), f32),
            pltpu.VMEM((owners, r, LANES), f32),
            pltpu.VMEM((owners, r, LANES), f32),
            pltpu.VMEM((meta_rows, LANES), f32),
            pltpu.VMEM((owners - 1, meta_rows, LANES), f32),
            pltpu.VMEM((old_steps + 1, SUBLANES, LANES), f32),
            pltpu.VMEM((old_steps, SUBLANES, LANES), f32),
            pltpu.VMEM((ITERS, owners, r, LANES), f32),
            pltpu.VMEM((ITERS, owners - 1, owners, r, LANES), f32),
            pltpu.SemaphoreType.DMA((3,)),
            pltpu.SemaphoreType.DMA((8,)),
            pltpu.SemaphoreType.DMA((8,)),
            pltpu.SemaphoreType.DMA((owners - 1,)),
            pltpu.SemaphoreType.DMA((owners - 1,)),
            pltpu.SemaphoreType.DMA((old_steps,)),
            pltpu.SemaphoreType.DMA((old_steps,)),
            pltpu.SemaphoreType.DMA((ITERS, owners - 1, owners)),
            pltpu.SemaphoreType.DMA((ITERS, owners - 1, owners)),
        ],
        compiler_params=pltpu.CompilerParams(
            collective_id=0, has_side_effects=True, vmem_limit_bytes=56 * 2**20
        ),
    )(
        centroids_old,
        centroids_new.reshape(2, half, depth),
        mass_old.reshape(n_old // LANES, LANES),
        mass_new.reshape(r, LANES),
    )
    log_old, log_new = pl.pallas_call(
        log_kernel,
        out_shape=(
            jax.ShapeDtypeStruct(left.shape, f32),
            jax.ShapeDtypeStruct(scales.shape, f32),
        ),
    )(left, scales)
    return log_old.reshape(-1), log_new.reshape(-1)


def solution(mesh):
    def body(centroids_old, centroids_new, mass_old, mass_new, pairs):
        group_blocks = mesh.shape["new"] * centroids_new.shape[0] // CENTROID_BLOCK
        olds = mesh.shape["old"]
        if group_blocks == PARTNER_BLOCKS and mesh.shape["new"] == 4 and olds & (olds - 1) == 0:
            return dense_body(mesh, centroids_old, centroids_new, mass_old, mass_new)
        return general_body(centroids_old, centroids_new, mass_old, mass_new, pairs)

    return jax.shard_map(
        body,
        mesh=mesh,
        in_specs=(
            P(("old", "new"), None),
            P(("old", "new"), None),
            P(("old", "new")),
            P(("old", "new")),
            P(("old", "new"), None),
        ),
        out_specs=(P(("old", "new")), P(("old", "new"))),
        check_vma=False,
    )
```

profile of v0, /device:TPU:0, one launch (start us, length us, event | category | flops | bytes accessed | tf_op | source)
XLA Modules:
  0.0 52.8 jit_solution(7617499492623159467)
XLA Ops:
  0.6 50.9 %shard_map.59 = (f32[16,128]{1,0:T(8,128)}, f32[4,128]{1,0:T(4,128)}) custom-call(bf16[2048,768]{1,0:T(8,128)(2,1)} %old_hbm.1, bf16[2,256,768]{2,1,0:T(8,128)(2,1)} %bitcast.5, f32[16,128]{1,0:T(8,128)} %bitcast.6, f32[4,128]{1,0:T(4,128)} %bitcast.7), custom_call_target="tpu_custom_call" | custom-call | tf_op jit(solution)/shard_map/pallas_call | solution.py:429
  51.5 1.3 %shard_map.60 = (f32[16,128]{1,0:T(8,128)}, f32[4,128]{1,0:T(4,128)}) custom-call(f32[16,128]{1,0:T(8,128)} %get-tuple-element.6.left_ref, f32[4,128]{1,0:T(4,128)} %get-tuple-element.7.scales_ref), custom_call_target="tpu_custom_call" | custom-call | tf_op jit(solution)/shard_map/pallas_call | solution.py:481
where the time goes:
time: 53.1 us; the launch traced here: 52.8 us
  Pallas kernels  52.2 us (98%)
  between operations  0.64 us (1%)
    pallas_call x1, Pallas kernels, dense_body(): pl.pallas_call(functools.partial(dense_kernel, olds, olds * owners), out_...  50.9 us
    pallas_call x1, Pallas kernels, dense_body(): pl.pallas_call(log_kernel, out_shape=(jax.ShapeDtypeStruct(left.shape, f3...  1.31 us

commit v1 on v0

--- a/solution.py
+++ b/solution.py
@@ -103,10 +103,12 @@
     devices_all,
     old_hbm,
     new_hbm,
+    mass_old_hbm,
+    mass_new_hbm,
+    left_ref,
+    scales_ref,
     mass_old_ref,
     mass_new_ref,
-    left_ref,
-    scales_ref,
     a_ref,
     b_ref,
     k_ref,
@@ -157,19 +159,17 @@
     load_b = [
         pltpu.make_async_copy(new_hbm.at[h], b_ref.at[0, h], load_sem.at[1 + h]) for h in range(2)
     ]
-    load_a.start()
-    for copy in load_b:
-        copy.start()
-
-    meta[...] = jnp.zeros_like(meta)
-    meta[0:r, :] = mass_new_ref[...]
-    meta[r : r + 1, :] = jnp.sum(mass_old_ref[...], axis=0, keepdims=True)
-
+    load_mass = [
+        pltpu.make_async_copy(mass_old_hbm, mass_old_ref, load_sem.at[3]),
+        pltpu.make_async_copy(mass_new_hbm, mass_new_ref, load_sem.at[4]),
+    ]
     barrier = pltpu.get_barrier_semaphore()
     for p in range(1, 4):
         pl.semaphore_signal(barrier, inc=1, device_id={"new": peers[p]}, device_id_type=MESH)
     for peer in old_peers:
         pl.semaphore_signal(barrier, inc=1, device_id={"old": peer}, device_id_type=MESH)
+    for copy in load_mass + [load_a] + load_b:
+        copy.start()
     pl.semaphore_wait(barrier, 3 + len(old_peers))
 
     meta_copies = [
@@ -183,8 +183,6 @@
         )
         for p in range(1, 4)
     ]
-    for copy in meta_copies:
-        copy.start()
 
     def send(index, src, slot, h, p, part=None):
         return pltpu.make_async_remote_copy(
@@ -205,9 +203,21 @@
     quarters = [pl.ds(q * (half // 2), half // 2) for q in range(2)]
     relay_x = [send(4 + q, b_ref.at[2, 0, quarters[q]], 3, 0, 1, quarters[q]) for q in range(2)]
     relay_y = [send(6 + q, b_ref.at[1, 1, quarters[q]], 3, 1, 2, quarters[q]) for q in range(2)]
-    for index in (0, 2, 1, 3):
-        moves[index].start()
-
+    core = lax.rem(my_old, 2)
+
+    def start_moves():
+        for index in (0, 2, 1, 3):
+            moves[index].start()
+
+    pl.when(core == 0)(start_moves)
+
+    for copy in load_mass:
+        copy.wait()
+    meta[...] = jnp.zeros_like(meta)
+    meta[0:r, :] = mass_new_ref[...]
+    meta[r : r + 1, :] = jnp.sum(mass_old_ref[...], axis=0, keepdims=True)
+    for copy in meta_copies:
+        copy.start()
     load_a.wait()
 
     @pl.loop(0, tiles)
@@ -257,16 +267,6 @@
 
     for copy in load_b:
         copy.wait()
-    for copy in meta_copies:
-        copy.wait()
-    old_sum = meta[r : r + 1, :]
-    new_sum = jnp.sum(meta[0:r, :], axis=0, keepdims=True)
-    for p in range(1, 4):
-        old_sum = old_sum + meta_in[p - 1, r : r + 1, :]
-        new_sum = new_sum + jnp.sum(meta_in[p - 1, 0:r, :], axis=0, keepdims=True)
-    sums[0] = jnp.zeros((SUBLANES, LANES), jnp.float32)
-    sums[0, 0:1, :] = old_sum
-    sums[0, 1:2, :] = new_sum
     sums_copies = [
         pltpu.make_async_remote_copy(
             src_ref=sums.at[k],
@@ -285,20 +285,29 @@
         if k + 1 < old_steps:
             sums_copies[k + 1].start()
 
-    sums_copies[0].start()
     stage(((0, 0), (0, 1)), True)
+    pl.when(core == 1)(start_moves)
     moves[0].wait_recv()
     for copy in relay_y:
         copy.start()
     moves[2].wait_recv()
     for copy in relay_x:
         copy.start()
-    advance(0)
     stage(((1, 1), (2, 0)), False)
-    advance(1)
     moves[1].wait_recv()
     moves[3].wait_recv()
     stage(((1, 0), (2, 1)), False)
+    for copy in meta_copies:
+        copy.wait()
+    old_sum = meta[r : r + 1, :]
+    new_sum = jnp.sum(meta[0:r, :], axis=0, keepdims=True)
+    for p in range(1, 4):
+        old_sum = old_sum + meta_in[p - 1, r : r + 1, :]
+        new_sum = new_sum + jnp.sum(meta_in[p - 1, 0:r, :], axis=0, keepdims=True)
+    sums[0] = jnp.zeros((SUBLANES, LANES), jnp.float32)
+    sums[0, 0:1, :] = old_sum
+    sums[0, 1:2, :] = new_sum
+    sums_copies[0].start()
     rel_new[0] = meta[0:r, :] * scale
     for p in range(1, 4):
         rel_new[p] = meta_in[p - 1, 0:r, :] * scale
@@ -375,7 +384,7 @@
                 copies.append(exchange(sweep, 0, p, p))
                 copies[-1].start()
             total = col_sums(0)
-            for k in range(2, old_steps):
+            for k in range(ITERS - 1, old_steps):
                 advance(k)
             totals = jnp.sum(sums[old_steps], axis=1, keepdims=True)
             alpha = n_old * devices_all / totals[0:1, :]
@@ -400,6 +409,8 @@
                 copies.append([exchange(sweep, owner, p, owner) for p in (3, 2, 1)])
                 for copy in copies[-1]:
                     copy.start()
+            if sweep < old_steps:
+                advance(sweep)
             for owner in range(4):
                 for copy in copies[owner]:
                     copy.wait()
@@ -429,20 +440,22 @@
     left, scales = pl.pallas_call(
         functools.partial(dense_kernel, olds, olds * owners),
         out_shape=(
-            jax.ShapeDtypeStruct((n_old // LANES, LANES), f32),
-            jax.ShapeDtypeStruct((r, LANES), f32),
+            pltpu.VMEM((n_old // LANES, LANES), f32),
+            pltpu.VMEM((r, LANES), f32),
         ),
         in_specs=[
             pl.BlockSpec(memory_space=pl.ANY),
             pl.BlockSpec(memory_space=pl.ANY),
-            pl.BlockSpec(memory_space=pltpu.VMEM),
-            pl.BlockSpec(memory_space=pltpu.VMEM),
+            pl.BlockSpec(memory_space=pl.ANY),
+            pl.BlockSpec(memory_space=pl.ANY),
         ],
         out_specs=(
             pl.BlockSpec(memory_space=pltpu.VMEM),
             pl.BlockSpec(memory_space=pltpu.VMEM),
         ),
         scratch_shapes=[
+            pltpu.VMEM((n_old // LANES, LANES), f32),
+            pltpu.VMEM((r, LANES), f32),
             pltpu.VMEM((n_old, depth), jnp.bfloat16),
             pltpu.VMEM((owners, 2, half, depth), jnp.bfloat16),
             pltpu.VMEM((2 * owners, n_old, half), f32),
@@ -459,7 +472,7 @@
             pltpu.VMEM((old_steps, SUBLANES, LANES), f32),
             pltpu.VMEM((ITERS, owners, r, LANES), f32),
             pltpu.VMEM((ITERS, owners - 1, owners, r, LANES), f32),
-            pltpu.SemaphoreType.DMA((3,)),
+            pltpu.SemaphoreType.DMA((5,)),
             pltpu.SemaphoreType.DMA((8,)),
             pltpu.SemaphoreType.DMA((8,)),
             pltpu.SemaphoreType.DMA((owners - 1,)),
@@ -484,7 +497,9 @@
             jax.ShapeDtypeStruct(left.shape, f32),
             jax.ShapeDtypeStruct(scales.shape, f32),
         ),
-    )(left, scales)
+        in_specs=[pl.BlockSpec(memory_space=pltpu.VMEM)] * 2,
+        out_specs=[pl.BlockSpec(memory_space=pltpu.VMEM)] * 2,
+    )(pltpu.with_memory_space_constraint(left, pltpu.VMEM), pltpu.with_memory_space_constraint(scales, pltpu.VMEM))
     return log_old.reshape(-1), log_new.reshape(-1)
 
 

time: 53.1 us -> 49.9 us (0.940)
  Pallas kernels: 52.2 us -> 49.1 us
    pallas_call x1, Pallas kernels: 50.9 us -> 48.5 us  [dense_body(): pl.pallas_call(functools.partial(dense_kernel, olds, olds * owners), out_...]
    pallas_call x1, Pallas kernels: 1.31 us -> 0.61 us  [dense_body(): pl.pallas_call(log_kernel, out_shape=(jax.ShapeDtypeStruct(left.shape, f3...]
where the time goes in v1:
time: 49.9 us; the launch traced here: 49.7 us
  Pallas kernels  49.1 us (98%)
  between operations  0.64 us (1%)
    pallas_call x1, Pallas kernels, dense_body(): pl.pallas_call(functools.partial(dense_kernel, olds, olds * owners), out_...  48.5 us

profile of v1, /device:TPU:0, one launch (start us, length us, event | category | flops | bytes accessed | tf_op | source)
XLA Modules:
  0.0 49.7 jit_solution(5357334942211921805)
XLA Ops:
  0.6 48.5 %shard_map.59 = (f32[16,128]{1,0:T(8,128)S(1)}, f32[4,128]{1,0:T(4,128)S(1)}) custom-call(bf16[2048,768]{1,0:T(8,128)(2,1)} %old_hbm.1, bf16[2,256,768]{2,1,0:T(8,128)(2,1)} %bitcast.5, f32[16,128]{1,0:T(8,128)} %bitcast.6, f32[4,128]{1,0:T(4,128)} %bitcast.7), custom_call_target="tpu_custom_call" | custom-call | tf_op jit(solution)/shard_map/pallas_call | solution.py:440
  49.1 0.6 %shard_map.60 = (f32[16,128]{1,0:T(8,128)}, f32[4,128]{1,0:T(4,128)}) custom-call(f32[16,128]{1,0:T(8,128)S(1)} %get-tuple-element.6.left_ref, f32[4,128]{1,0:T(4,128)S(1)} %get-tuple-element.7.scales_ref), custom_call_target="tpu_custom_call" | custom-call | tf_op jit(solution)/shard_map/pallas_call | solution.py:494

commit v2 on v1

--- a/solution.py
+++ b/solution.py
@@ -140,10 +140,9 @@
     flip_x = 1 - 2 * lax.rem(me, 2)
     flip_y = 2 - 4 * lax.div(me, 2)
     peers = (None, me + flip_x, me + flip_y, me + flip_x + flip_y)
-    old_steps = olds.bit_length() - 1
-    old_peers = [
-        my_old + (1 << k) - (2 << k) * lax.rem(lax.div(my_old, 1 << k), 2) for k in range(old_steps)
-    ]
+    chips = olds // 2
+    core, chip = lax.rem(my_old, 2), lax.div(my_old, 2)
+    partner = my_old + 1 - 2 * core
 
     n_old = a_ref.shape[0]
     half = b_ref.shape[2]
@@ -166,11 +165,21 @@
     barrier = pltpu.get_barrier_semaphore()
     for p in range(1, 4):
         pl.semaphore_signal(barrier, inc=1, device_id={"new": peers[p]}, device_id_type=MESH)
-    for peer in old_peers:
-        pl.semaphore_signal(barrier, inc=1, device_id={"old": peer}, device_id_type=MESH)
+    pl.semaphore_signal(barrier, inc=1, device_id={"old": partner}, device_id_type=MESH)
+
+    @pl.when(chip > 0)
+    def _():
+        pl.semaphore_signal(barrier, inc=1, device_id={"old": my_old - 2}, device_id_type=MESH)
+
+    @pl.when(chip < chips - 1)
+    def _():
+        pl.semaphore_signal(barrier, inc=1, device_id={"old": my_old + 2}, device_id_type=MESH)
+
     for copy in load_mass + [load_a] + load_b:
         copy.start()
-    pl.semaphore_wait(barrier, 3 + len(old_peers))
+    ends = lax.convert_element_type(chip > 0, jnp.int32)
+    ends = ends + lax.convert_element_type(chip < chips - 1, jnp.int32)
+    pl.semaphore_wait(barrier, 4 + ends)
 
     meta_copies = [
         pltpu.make_async_remote_copy(
@@ -203,13 +212,13 @@
     quarters = [pl.ds(q * (half // 2), half // 2) for q in range(2)]
     relay_x = [send(4 + q, b_ref.at[2, 0, quarters[q]], 3, 0, 1, quarters[q]) for q in range(2)]
     relay_y = [send(6 + q, b_ref.at[1, 1, quarters[q]], 3, 1, 2, quarters[q]) for q in range(2)]
-    core = lax.rem(my_old, 2)
-
-    def start_moves():
-        for index in (0, 2, 1, 3):
-            moves[index].start()
-
-    pl.when(core == 0)(start_moves)
+
+    def start(copies):
+        def begin():
+            for copy in copies:
+                copy.start()
+
+        return begin
 
     for copy in load_mass:
         copy.wait()
@@ -218,6 +227,8 @@
     meta[r : r + 1, :] = jnp.sum(mass_old_ref[...], axis=0, keepdims=True)
     for copy in meta_copies:
         copy.start()
+    start([moves[0], moves[2]])()
+    pl.when(core == 0)(start([moves[1], moves[3]]))
     load_a.wait()
 
     @pl.loop(0, tiles)
@@ -267,47 +278,81 @@
 
     for copy in load_b:
         copy.wait()
-    sums_copies = [
-        pltpu.make_async_remote_copy(
-            src_ref=sums.at[k],
-            dst_ref=sums_in.at[k],
-            send_sem=sums_send.at[k],
-            recv_sem=sums_recv.at[k],
-            device_id={"old": peer},
+    pair_copy = pltpu.make_async_remote_copy(
+        src_ref=sums.at[0],
+        dst_ref=sums.at[1],
+        send_sem=sums_send.at[0],
+        recv_sem=sums_recv.at[0],
+        device_id={"old": partner},
+        device_id_type=MESH,
+    )
+
+    def flood_copy(side, k):
+        index = 1 + 2 * k + side
+        return pltpu.make_async_remote_copy(
+            src_ref=sums.at[2] if k == 0 else sums_in.at[side, k - 1],
+            dst_ref=sums_in.at[side, k],
+            send_sem=sums_send.at[index],
+            recv_sem=sums_recv.at[index],
+            device_id={"old": my_old + 2 - 4 * side},
             device_id_type=MESH,
         )
-        for k, peer in enumerate(old_peers)
-    ]
-
-    def advance(k):
-        sums_copies[k].wait()
-        sums[k + 1] = sums[k] + sums_in[k]
-        if k + 1 < old_steps:
-            sums_copies[k + 1].start()
+
+    def sends(side, k):
+        here = chip if side == 0 else chips - 1 - chip
+        return jnp.logical_and(here < chips - 1, here >= k)
+
+    def receives(side, k):
+        here = chip if side == 0 else chips - 1 - chip
+        return here > k
+
+    def advance(step):
+        if step == 0:
+            for copy in meta_copies:
+                copy.wait()
+            old_sum = meta[r : r + 1, :]
+            new_sum = jnp.sum(meta[0:r, :], axis=0, keepdims=True)
+            for p in range(1, 4):
+                old_sum = old_sum + meta_in[p - 1, r : r + 1, :]
+                new_sum = new_sum + jnp.sum(meta_in[p - 1, 0:r, :], axis=0, keepdims=True)
+            sums[0] = jnp.zeros((SUBLANES, LANES), jnp.float32)
+            sums[0, 0:1, :] = old_sum
+            sums[0, 1:2, :] = new_sum
+            pair_copy.start()
+        elif step == 1:
+            pair_copy.wait()
+            sums[2] = sums[0] + sums[1]
+            sums[3] = sums[2]
+        if 1 < step <= chips:
+            for side in range(2):
+
+                @pl.when(receives(side, step - 2))
+                def _():
+                    flood_copy(side, step - 2).wait_recv()
+                    sums[3] = sums[3] + sums_in[side, step - 2]
+
+        if 1 <= step < chips:
+            for side in range(2):
+                pl.when(sends(side, step - 1))(flood_copy(side, step - 1).start)
+
+    def finish_floods():
+        for k in range(chips - 1):
+            for side in range(2):
+                pl.when(sends(side, k))(flood_copy(side, k).wait_send)
 
     stage(((0, 0), (0, 1)), True)
-    pl.when(core == 1)(start_moves)
+    advance(0)
     moves[0].wait_recv()
-    for copy in relay_y:
-        copy.start()
+    pl.when(core == 0)(start(relay_y))
     moves[2].wait_recv()
-    for copy in relay_x:
-        copy.start()
+    pl.when(core == 0)(start(relay_x))
     stage(((1, 1), (2, 0)), False)
+    pl.when(core == 1)(start([moves[1], moves[3]] + relay_y + relay_x))
+    advance(1)
     moves[1].wait_recv()
     moves[3].wait_recv()
     stage(((1, 0), (2, 1)), False)
-    for copy in meta_copies:
-        copy.wait()
-    old_sum = meta[r : r + 1, :]
-    new_sum = jnp.sum(meta[0:r, :], axis=0, keepdims=True)
-    for p in range(1, 4):
-        old_sum = old_sum + meta_in[p - 1, r : r + 1, :]
-        new_sum = new_sum + jnp.sum(meta_in[p - 1, 0:r, :], axis=0, keepdims=True)
-    sums[0] = jnp.zeros((SUBLANES, LANES), jnp.float32)
-    sums[0, 0:1, :] = old_sum
-    sums[0, 1:2, :] = new_sum
-    sums_copies[0].start()
+    advance(2)
     rel_new[0] = meta[0:r, :] * scale
     for p in range(1, 4):
         rel_new[p] = meta_in[p - 1, 0:r, :] * scale
@@ -384,9 +429,10 @@
                 copies.append(exchange(sweep, 0, p, p))
                 copies[-1].start()
             total = col_sums(0)
-            for k in range(ITERS - 1, old_steps):
-                advance(k)
-            totals = jnp.sum(sums[old_steps], axis=1, keepdims=True)
+            for step in range(ITERS + 2, chips + 1):
+                advance(step)
+            finish_floods()
+            totals = jnp.sum(sums[3], axis=1, keepdims=True)
             alpha = n_old * devices_all / totals[0:1, :]
             beta = r * LANES * devices_all / totals[1:2, :]
             ratio = alpha / beta
@@ -409,8 +455,7 @@
                 copies.append([exchange(sweep, owner, p, owner) for p in (3, 2, 1)])
                 for copy in copies[-1]:
                     copy.start()
-            if sweep < old_steps:
-                advance(sweep)
+            advance(3 + sweep)
             for owner in range(4):
                 for copy in copies[owner]:
                     copy.wait()
@@ -434,7 +479,7 @@
     n_new = centroids_new.shape[0]
     half = n_new // 2
     r = n_new // LANES
-    old_steps = olds.bit_length() - 1
+    chips = olds // 2
     f32 = jnp.float32
     meta_rows = -(-(r + 1) // SUBLANES) * SUBLANES
     left, scales = pl.pallas_call(
@@ -468,8 +513,8 @@
             pltpu.VMEM((owners, r, LANES), f32),
             pltpu.VMEM((meta_rows, LANES), f32),
             pltpu.VMEM((owners - 1, meta_rows, LANES), f32),
-            pltpu.VMEM((old_steps + 1, SUBLANES, LANES), f32),
-            pltpu.VMEM((old_steps, SUBLANES, LANES), f32),
+            pltpu.VMEM((4, SUBLANES, LANES), f32),
+            pltpu.VMEM((2, max(chips - 1, 1), SUBLANES, LANES), f32),
             pltpu.VMEM((ITERS, owners, r, LANES), f32),
             pltpu.VMEM((ITERS, owners - 1, owners, r, LANES), f32),
             pltpu.SemaphoreType.DMA((5,)),
@@ -477,8 +522,8 @@
             pltpu.SemaphoreType.DMA((8,)),
             pltpu.SemaphoreType.DMA((owners - 1,)),
             pltpu.SemaphoreType.DMA((owners - 1,)),
-            pltpu.SemaphoreType.DMA((old_steps,)),
-            pltpu.SemaphoreType.DMA((old_steps,)),
+            pltpu.SemaphoreType.DMA((2 * chips + 1,)),
+            pltpu.SemaphoreType.DMA((2 * chips + 1,)),
             pltpu.SemaphoreType.DMA((ITERS, owners - 1, owners)),
             pltpu.SemaphoreType.DMA((ITERS, owners - 1, owners)),
         ],
@@ -507,7 +552,7 @@
     def body(centroids_old, centroids_new, mass_old, mass_new, pairs):
         group_blocks = mesh.shape["new"] * centroids_new.shape[0] // CENTROID_BLOCK
         olds = mesh.shape["old"]
-        if group_blocks == PARTNER_BLOCKS and mesh.shape["new"] == 4 and olds & (olds - 1) == 0:
+        if group_blocks == PARTNER_BLOCKS and mesh.shape["new"] == 4 and olds % 2 == 0:
             return dense_body(mesh, centroids_old, centroids_new, mass_old, mass_new)
         return general_body(centroids_old, centroids_new, mass_old, mass_new, pairs)
 

time: 49.9 us -> 47.7 us (0.956)
  Pallas kernels: 49.1 us -> 46.8 us
    pallas_call x1, Pallas kernels: 48.5 us -> 46.2 us  [dense_body(): pl.pallas_call(functools.partial(dense_kernel, olds, olds * owners), out_...]
where the time goes in v2:
time: 47.7 us; the launch traced here: 47.5 us
  Pallas kernels  46.8 us (98%)
  between operations  0.64 us (1%)
    pallas_call x1, Pallas kernels, dense_body(): pl.pallas_call(functools.partial(dense_kernel, olds, olds * owners), out_...  46.2 us

profile of v2, /device:TPU:0, one launch (start us, length us, event | category | flops | bytes accessed | tf_op | source)
XLA Modules:
  0.0 47.5 jit_solution(17525482027952458946)
XLA Ops:
  0.6 46.2 %shard_map.59 = (f32[16,128]{1,0:T(8,128)S(1)}, f32[4,128]{1,0:T(4,128)S(1)}) custom-call(bf16[2048,768]{1,0:T(8,128)(2,1)} %old_hbm.1, bf16[2,256,768]{2,1,0:T(8,128)(2,1)} %bitcast.5, f32[16,128]{1,0:T(8,128)} %bitcast.6, f32[4,128]{1,0:T(4,128)} %bitcast.7), custom_call_target="tpu_custom_call" | custom-call | tf_op jit(solution)/shard_map/pallas_call | solution.py:485
  46.9 0.6 %shard_map.60 = (f32[16,128]{1,0:T(8,128)}, f32[4,128]{1,0:T(4,128)}) custom-call(f32[16,128]{1,0:T(8,128)S(1)} %get-tuple-element.6.left_ref, f32[4,128]{1,0:T(4,128)S(1)} %get-tuple-element.7.scales_ref), custom_call_target="tpu_custom_call" | custom-call | tf_op jit(solution)/shard_map/pallas_call | solution.py:539
